TPU v7x, 32 devices: a whole 2x2x4 slice. The times are simulated.
32 devices in a mesh: region: 8 (over y, x, core), group: 4 (over z).
Axes of the slice: x: 2, y: 2, z: 4, core: 2. Of those that a mesh axis runs over, the one named last changes fastest.
Arguments:
- ensemble: bfloat16 [8192, 512], P(('region', 'group')), may hold values from -6 to 6
- tiles: bfloat16 [2, 256, 8192], P(None, None, ('region', 'group')), may hold values from -0.09375 to 0.09375
- tile_live: int32 [2, 8], replicated, may hold values 0 or 1
- observed: float32 [2, 256], replicated, may hold values from -6 to 6
- perturb: bfloat16 [2, 256, 512], replicated, may hold values from -6 to 6
- obs_var: float32 [2, 256], replicated, may hold values from 0.5 to 4
Outputs:
- analysis: bfloat16 [8192, 512], P(('region', 'group'))
All inputs are finite; a program needn't handle non-finite values. Where the computation divides by a largest or mean magnitude, that divisor is 1e-20 or more.
Results may differ from a plain program's by a relative error of at most 0.013.
Values may be sent and summed in bfloat16 or wider, within the bound.
A program may use at most 64 MiB of HBM per device.

v0:
```python
import jax
import jax.numpy as jnp
from jax import lax
from jax.sharding import PartitionSpec as P

M = 512
P_SIZE = 256
BATCHES = 2
NEWTON = 4


def newton_weights(spread, innov, var_row):
    cov = jnp.dot(spread, spread.T, precision=lax.Precision.HIGHEST) / (M - 1) + jnp.diag(var_row)
    bound = jnp.max(jnp.sum(jnp.abs(cov), axis=1))
    ident = jnp.eye(P_SIZE, dtype=jnp.float32)
    approx = ident / bound
    for step in range(NEWTON):
        inner = 2.0 * ident - jnp.dot(cov, approx, precision=lax.Precision.HIGHEST)
        approx = jnp.dot(approx, inner, precision=lax.Precision.HIGHEST)
    return jnp.dot(approx, innov, precision=lax.Precision.HIGHEST).astype(jnp.bfloat16)


def on_device(ensemble, tiles, tile_live, observed, perturb, obs_var):
    region_index = lax.axis_index("region")
    group_index = lax.axis_index("group")
    group_count = lax.axis_size("group")
    share_rows = P_SIZE // group_count
    state = ensemble
    for batch in range(BATCHES):
        flag = lax.dynamic_index_in_dim(tile_live[batch], region_index, keepdims=False)
        operator = tiles[batch]
        current = state
        partial_value = lax.cond(
            flag > 0,
            lambda: jnp.dot(operator, current, preferred_element_type=jnp.float32),
            lambda: jnp.zeros((operator.shape[0], current.shape[1]), jnp.float32),
        )
        obs_row = observed[batch]
        perturb_b = perturb[batch].astype(jnp.float32)
        var_row = obs_var[batch]
        within = lax.psum_scatter(partial_value, "group", scatter_dimension=0, tiled=True)
        share = lax.psum(within, "region")
        start = group_index * share_rows
        obs_share = lax.dynamic_slice_in_dim(obs_row, start, share_rows, 0)
        perturb_share = lax.dynamic_slice_in_dim(perturb_b, start, share_rows, 0)
        spread_share = share - jnp.mean(share, axis=1, keepdims=True)
        innov_share = obs_share[:, None] + perturb_share - share
        spread, innov = (
            lax.all_gather(spread_share, "group", axis=0, tiled=True),
            lax.all_gather(innov_share, "group", axis=0, tiled=True),
        )
        spread_low = spread.astype(jnp.bfloat16)
        weights = newton_weights(spread, innov, var_row)
        wide = state.astype(jnp.float32)
        anom = (wide - jnp.mean(wide, axis=1, keepdims=True)).astype(jnp.bfloat16)
        gain = (jnp.dot(anom, spread_low.T, preferred_element_type=jnp.float32) / (M - 1)).astype(
            jnp.bfloat16
        )
        state = (wide + jnp.dot(gain, weights, preferred_element_type=jnp.float32)).astype(
            jnp.bfloat16
        )
    return state


def solution(mesh):
    return jax.shard_map(
        on_device,
        mesh=mesh,
        in_specs=(
            P(("region", "group"), None),
            P(None, None, ("region", "group")),
            P(),
            P(),
            P(),
            P(),
        ),
        out_specs=P(("region", "group"), None),
        check_vma=False,
    )
```

profile of v0, /device:TPU:0, one launch (start us, length us, event | category | flops | bytes accessed | tf_op | source)
XLA Modules:
  0.0 254.0 jit_solution(17412516982273053255)
XLA Ops:
  6.5 0.7 copy-done.9
  7.2 0.6 fusion.56
  8.4 1.3 conditional.2
  8.4 1.3 fusion
  9.7 0.8 copy-done.1
  11.4 0.7 copy-done.7
  12.0 0.7 copy-done.8
  12.8 22.5 %reduce-scatter.3.cloned.1.call-done = f32[64,512]{1,0:T(8,128)} async-done(((f32[256,512]{1,0:T(8,128)}), f32[64,512]{1,0:T(8,128)}) %reduce-scatter.3.cloned.1.call-update) | async-done | bytes 131088 | tf_op jit(solution)/shard_map/reduce_scatter | solution.py:41
  35.4 54.6 %all-reduce.3.cloned.1.call-done = f32[64,512]{1,0:T(8,128)} async-done(((f32[64,512]{1,0:T(8,128)}), f32[64,512]{1,0:T(8,128)}) %all-reduce.3.cloned.1.call-update) | async-done | bytes 131088 | tf_op jit(solution)/shard_map/psum | solution.py:42
  90.0 1.1 reduce_sum.55
  91.2 14.9 %all_gather.12 = f32[256,512]{1,0:T(8,128)S(1)} all-gather(f32[64,512]{1,0:T(8,128)S(1)} %get-tuple-element.32), channel_id=1, replica_groups=mesh['region'=8,'group'=4] {'group'}, dimensions={0}, use_global_device_ids=true | all-gather | bytes 655360 | tf_op jit(solution)/shard_map/all_gather | solution.py:49
  106.1 0.6 abs_reduce_fusion.1
  106.8 0.6 reduce_max.18
  108.9 0.6 convolution_subtract_fusion.6
  109.9 0.6 convolution_subtract_fusion.5
  111.0 0.6 convolution_subtract_fusion.4
  112.0 16.1 %all_gather.13 = f32[256,512]{1,0:T(8,128)S(1)} all-gather(f32[64,512]{1,0:T(8,128)S(1)} %get-tuple-element.31), channel_id=1, replica_groups=mesh['region'=8,'group'=4] {'group'}, dimensions={0}, use_global_device_ids=true | all-gather | bytes 655360 | tf_op jit(solution)/shard_map/all_gather | solution.py:50
  128.0 0.6 convolution_convert_fusion.1
  128.7 0.8 convert_reduce_fusion
  129.9 0.8 copy-done.2
  130.8 21.8 %reduce-scatter.5.cloned.1.call-done = f32[64,512]{1,0:T(8,128)} async-done(((f32[256,512]{1,0:T(8,128)}), f32[64,512]{1,0:T(8,128)}) %reduce-scatter.5.cloned.1.call-update) | async-done | bytes 131088 | tf_op jit(solution)/shard_map/reduce_scatter | solution.py:41
  152.7 54.7 %all-reduce.5.cloned.1.call-done = f32[64,512]{1,0:T(8,128)} async-done(((f32[64,512]{1,0:T(8,128)}), f32[64,512]{1,0:T(8,128)}) %all-reduce.5.cloned.1.call-update) | async-done | bytes 131088 | tf_op jit(solution)/shard_map/psum | solution.py:42
  207.4 1.1 reduce_sum.58
  208.6 14.9 %all_gather.14 = f32[256,512]{1,0:T(8,128)S(1)} all-gather(f32[64,512]{1,0:T(8,128)S(1)} %get-tuple-element.30), channel_id=1, replica_groups=mesh['region'=8,'group'=4] {'group'}, dimensions={0}, use_global_device_ids=true | all-gather | bytes 655360 | tf_op jit(solution)/shard_map/all_gather | solution.py:49
  223.5 0.6 abs_reduce_fusion
  224.1 0.6 reduce_max.19
  226.2 0.6 convolution_subtract_fusion.2
  227.3 0.6 convolution_subtract_fusion.1
  228.3 0.6 convolution_subtract_fusion
  229.3 16.1 %all_gather.15 = f32[256,512]{1,0:T(8,128)S(1)} all-gather(f32[64,512]{1,0:T(8,128)S(1)} %get-tuple-element.29), channel_id=1, replica_groups=mesh['region'=8,'group'=4] {'group'}, dimensions={0}, use_global_device_ids=true | all-gather | bytes 655360 | tf_op jit(solution)/shard_map/all_gather | solution.py:50
  245.4 0.6 convolution_convert_fusion
  246.0 1.4 fusion.7
  (48 shorter events, 5.4 us)
Async XLA Ops:
  6.5 28.7 %reduce-scatter.3.cloned.1.call-start = ((), (), s32[]{:S(2)}) async-start(), calls=%async_computation.2 | async-start | bytes 655360 | tf_op jit(solution)/shard_map/reduce_scatter | solution.py:41
  6.5 0.7 copy-start.9
  8.4 4.3 %copy-start.3 = (bf16[2,256,512]{2,1,0:T(8,128)(2,1)S(1)}, bf16[2,256,512]{2,1,0:T(8,128)(2,1)}, u32[]{:S(2)}) copy-start(bf16[2,256,512]{2,1,0:T(8,128)(2,1)} %param.14) | copy-start | bytes 1572868
  9.7 0.8 copy-start.1
  9.7 1.5 copy-start
  10.5 79.5 %all-reduce.3.cloned.1.call-start = ((), (), s32[]{:S(2)}) async-start(), calls=%async_computation.3 | async-start | bytes 262144 | tf_op jit(solution)/shard_map/psum | solution.py:42
  11.3 0.7 copy-start.7
  12.0 0.7 copy-start.8
  35.3 117.4 %reduce-scatter.5.cloned.1.call-start = ((), (), s32[]{:S(2)}) async-start(), calls=%async_computation.4 | async-start | bytes 655360 | tf_op jit(solution)/shard_map/reduce_scatter | solution.py:41
  90.0 1.1 copy-start.5
  128.7 1.0 copy-start.6
  129.9 0.8 copy-start.2
  130.7 76.7 %all-reduce.5.cloned.1.call-start = ((), (), s32[]{:S(2)}) async-start(), calls=%async_computation.5 | async-start | bytes 262144 | tf_op jit(solution)/shard_map/psum | solution.py:42
  207.4 1.1 copy-start.4
Sparse Core Ops, SparseCore 0:
  10.6 24.5 reduce-scatter.2
  38.3 51.6 all-reduce.2
  130.8 21.8 reduce-scatter.4
  155.5 51.7 all-reduce.4
where the time goes:
time: 254 us
  waiting for transfers between devices  154 us (61%)
  blocking collectives  62 us (24%)
  between operations  16 us (6%)
  matrix products  13.9 us (5%)
  other arithmetic  4.28 us (2%)
  local copies, waits for them, and re-layouts  3.98 us (2%)
    psum x2, waiting for transfers between devices, on_device(): share = lax.psum(within, 'region')  109 us
    reduce_scatter x2, waiting for transfers between devices, on_device(): lax.psum_scatter(partial_value, 'group', scatter_dimension=0, tiled=True)  44.4 us
    all_gather x2, blocking collectives, on_device(): lax.all_gather(innov_share, 'group', axis=0, tiled=True)  32.1 us
    all_gather x2, blocking collectives, on_device(): lax.all_gather(spread_share, 'group', axis=0, tiled=True)  29.9 us
  transfers between devices with their start and end apart: 4, of which 4 were waited for; matrix products, arithmetic and copies ran while one was open for 0% of the time, Pallas kernels for 0%

commit v1 on v0

v1 whole, which is shorter than its diff:
```python
import functools

import jax
import jax.numpy as jnp
from jax import lax
from jax.experimental import pallas as pl
from jax.experimental.pallas import tpu as pltpu
from jax.sharding import PartitionSpec as P

NEWTON = 4
F32 = jnp.float32
BF16 = jnp.bfloat16


def split(x):
    hi = x.astype(BF16)
    return hi, (x - hi.astype(F32)).astype(BF16)


def dot3(a, b):
    left = jnp.concatenate([a[0], a[0], a[1]], axis=1)
    right = jnp.concatenate([b[0], b[1], b[0]], axis=0)
    return jnp.dot(left, right, preferred_element_type=F32)


def dot_nt(a, b):
    return lax.dot_general(a, b, (((1,), (1,)), ((), ())), preferred_element_type=F32)


def kernel(
    region_count, group_count,
    ens_hbm, tiles_hbm, live_ref, obs_ref, pert_hbm, var_ref,
    out_ref,
    ens, tiles, pert, partial, rs_buf, z_send, z_buf, spread_buf,
    mean_part, mean_rs, mean_zsend, mean_z,
    load_sem, rs_ssem, rs_rsem, z_ssem, z_rsem, ag_ssem, ag_rsem,
    mrs_ssem, mrs_rsem, mz_ssem, mz_rsem,
):
    batches, obs_count, members = pert.shape
    region = lax.axis_index("region")
    group = lax.axis_index("group")
    chunk_rows, chunk_cols = rs_buf.shape[2:]
    across = members // chunk_cols

    barrier = pltpu.get_barrier_semaphore()
    for k in range(1, region_count):
        pl.semaphore_signal(barrier, inc=1, device_id=(lax.rem(region + k, region_count), group), device_id_type=pl.DeviceIdType.MESH)
    for k in range(1, group_count):
        pl.semaphore_signal(barrier, inc=1, device_id=(region, lax.rem(group + k, group_count)), device_id_type=pl.DeviceIdType.MESH)

    loads = [pltpu.make_async_copy(ens_hbm, ens, load_sem.at[0])]
    loads += [pltpu.make_async_copy(tiles_hbm.at[b], tiles.at[b], load_sem.at[1 + b]) for b in range(batches)]
    loads += [pltpu.make_async_copy(pert_hbm.at[b], pert.at[b], load_sem.at[1 + batches + b]) for b in range(batches)]
    for load in loads:
        load.start()

    row_at = lax.broadcasted_iota(jnp.int32, (obs_count, obs_count), 0)
    col_at = lax.broadcasted_iota(jnp.int32, (obs_count, obs_count), 1)
    on_diag = row_at == col_at
    ident = jnp.where(on_diag, 1.0, 0.0).astype(F32)

    def as_row(column):
        return jnp.sum(jnp.where(on_diag, column, 0.0), axis=0, keepdims=True)

    def as_column(row):
        return jnp.sum(jnp.where(on_diag, row, 0.0), axis=1, keepdims=True)

    def chunk(ref, index):
        rows = pl.ds(pl.multiple_of(lax.div(index, across) * chunk_rows, chunk_rows), chunk_rows)
        if across == 1:
            return ref.at[rows, :]
        return ref.at[rows, pl.ds(pl.multiple_of(lax.rem(index, across) * chunk_cols, chunk_cols), chunk_cols)]

    def remote(src, dst, ssem, rsem, where):
        return pltpu.make_async_remote_copy(
            src_ref=src, dst_ref=dst, send_sem=ssem, recv_sem=rsem,
            device_id=where, device_id_type=pl.DeviceIdType.MESH,
        )

    region_peers = [lax.rem(region + k, region_count) for k in range(1, region_count)]
    group_peers = [lax.rem(group + k, group_count) for k in range(1, group_count)]
    sends = []

    def launch(copy):
        copy.start()
        sends.append(copy)

    def local_partial(b):
        loads[1 + b].wait()
        value = jnp.dot(tiles[b], ens[...], preferred_element_type=F32)
        value = value * live_ref[b, region].astype(F32)
        mean = jnp.mean(value, axis=1, keepdims=True)
        partial[b] = (value - mean).astype(BF16)
        mean_part[:, b * obs_count:(b + 1) * obs_count] = as_row(mean)

    def scatter(b):
        for k, peer in enumerate(region_peers):
            launch(remote(chunk(partial.at[b], peer), rs_buf.at[b, region], rs_ssem.at[b, k], rs_rsem.at[b, region], (peer, group)))

    def sum_region(b):
        total = chunk(partial.at[b], region)[...].astype(F32)
        for peer in region_peers:
            remote(rs_buf.at[b, peer], rs_buf.at[b, peer], rs_ssem.at[b, 0], rs_rsem.at[b, peer], (peer, group)).wait_recv()
            total = total + rs_buf[b, peer].astype(F32)
        z_send[b] = total.astype(BF16)
        for k, peer in enumerate(group_peers):
            launch(remote(z_send.at[b], z_buf.at[b, group], z_ssem.at[b, k], z_rsem.at[b, group], (region, peer)))

    def sum_group(b):
        total = z_send[b].astype(F32)
        for peer in group_peers:
            remote(z_buf.at[b, peer], z_buf.at[b, peer], z_ssem.at[b, 0], z_rsem.at[b, peer], (region, peer)).wait_recv()
            total = total + z_buf[b, peer].astype(F32)
        mine = chunk(spread_buf.at[b], region)
        mine[...] = total.astype(BF16)
        for k, peer in enumerate(region_peers):
            launch(remote(mine, mine, ag_ssem.at[b, k], ag_rsem.at[b, region], (peer, group)))

    def gathered(b):
        for peer in region_peers:
            block = chunk(spread_buf.at[b], peer)
            remote(block, block, ag_ssem.at[b, 0], ag_rsem.at[b, peer], (peer, group)).wait_recv()
        return spread_buf[b]

    loads[0].wait()
    local_partial(0)
    pl.semaphore_wait(barrier, region_count - 1 + group_count - 1)
    scatter(0)
    for b in range(1, batches):
        local_partial(b)
    for k, peer in enumerate(region_peers):
        launch(remote(mean_part, mean_rs.at[region], mrs_ssem.at[k], mrs_rsem.at[region], (peer, group)))
    for b in range(1, batches):
        scatter(b)

    sum_region(0)
    total = mean_part[...]
    for peer in region_peers:
        remote(mean_rs.at[peer], mean_rs.at[peer], mrs_ssem.at[0], mrs_rsem.at[peer], (peer, group)).wait_recv()
        total = total + mean_rs[peer]
    mean_zsend[...] = total
    for k, peer in enumerate(group_peers):
        launch(remote(mean_zsend, mean_z.at[group], mz_ssem.at[k], mz_rsem.at[group], (region, peer)))
    for b in range(1, batches):
        sum_region(b)
    sum_group(0)
    mean_row = mean_zsend[...]
    for peer in group_peers:
        remote(mean_z.at[peer], mean_z.at[peer], mz_ssem.at[0], mz_rsem.at[peer], (region, peer)).wait_recv()
        mean_row = mean_row + mean_z[peer]
    for b in range(1, batches):
        sum_group(b)

    def anomaly(wide):
        return (wide - jnp.mean(wide, axis=1, keepdims=True)).astype(BF16)

    def newton_weights(spread_low, mismatch, shift, b):
        cov = dot_nt(spread_low, spread_low) / (members - 1) + jnp.where(on_diag, var_ref[b:b + 1, :], 0.0)
        bound = jnp.max(jnp.sum(jnp.abs(cov), axis=1, keepdims=True), axis=0, keepdims=True)
        residual = ident - cov / bound
        approx = ident + residual
        for step in range(1, NEWTON):
            parts = split(residual)
            residual = dot3(parts, parts)
            approx = approx + dot3(split(approx), split(residual))
        innov = mismatch + shift
        return (dot3(split(approx), split(innov)) / bound).astype(BF16)

    state = ens[...].astype(F32)
    anom = anomaly(state)
    offsets = [
        as_column(obs_ref[b:b + 1, :] - mean_row[:, b * obs_count:(b + 1) * obs_count]) for b in range(batches)
    ]
    history = []
    for b in range(batches):
        loads[1 + batches + b].wait()
        prior = gathered(b)
        spread = prior.astype(F32)
        for earlier_low, earlier_weights in history:
            base = spread - jnp.mean(spread, axis=1, keepdims=True)
            hi, lo = split(base)
            cross = split((dot_nt(hi, earlier_low) + dot_nt(lo, earlier_low)) / (members - 1))
            spread = spread + jnp.dot(cross[0], earlier_weights, preferred_element_type=F32)
            spread = spread + jnp.dot(cross[1], earlier_weights, preferred_element_type=F32)
        mismatch = pert[b].astype(F32) - spread
        if history:
            spread = spread - jnp.mean(spread, axis=1, keepdims=True)
        spread_low = spread.astype(BF16)
        gain = (dot_nt(anom, spread_low) / (members - 1)).astype(BF16)
        weights = newton_weights(spread_low, mismatch, offsets[b], b)
        low = (state + jnp.dot(gain, weights, preferred_element_type=F32)).astype(BF16)
        history.append((spread_low, weights))
        if b + 1 < batches:
            state = low.astype(F32)
            anom = anomaly(state)
    out_ref[...] = low
    for copy in sends:
        copy.wait_send()


def on_device(ensemble, tiles, tile_live, observed, perturb, obs_var):
    region_count = lax.axis_size("region")
    group_count = lax.axis_size("group")
    batches, obs_count, members = perturb.shape
    chunk_rows = max(16, obs_count // region_count)
    chunk_cols = obs_count * members // (region_count * chunk_rows)
    vmem = pl.BlockSpec(memory_space=pltpu.VMEM)
    hbm = pl.BlockSpec(memory_space=pl.ANY)
    block = (chunk_rows, chunk_cols)
    dma = pltpu.SemaphoreType.DMA
    return pl.pallas_call(
        functools.partial(kernel, region_count, group_count),
        out_shape=jax.ShapeDtypeStruct(ensemble.shape, ensemble.dtype),
        in_specs=[hbm, hbm, pl.BlockSpec(memory_space=pltpu.SMEM), vmem, hbm, vmem],
        out_specs=vmem,
        scratch_shapes=[
            pltpu.VMEM(ensemble.shape, BF16),
            pltpu.VMEM(tiles.shape, BF16),
            pltpu.VMEM(perturb.shape, BF16),
            pltpu.VMEM(perturb.shape, BF16),
            pltpu.VMEM((batches, region_count, *block), BF16),
            pltpu.VMEM((batches, *block), BF16),
            pltpu.VMEM((batches, group_count, *block), BF16),
            pltpu.VMEM(perturb.shape, BF16),
            pltpu.VMEM((1, batches * obs_count), F32),
            pltpu.VMEM((region_count, 1, batches * obs_count), F32),
            pltpu.VMEM((1, batches * obs_count), F32),
            pltpu.VMEM((group_count, 1, batches * obs_count), F32),
            dma((1 + 2 * batches,)),
            dma((batches, region_count)),
            dma((batches, region_count)),
            dma((batches, group_count)),
            dma((batches, group_count)),
            dma((batches, region_count)),
            dma((batches, region_count)),
            dma((region_count,)),
            dma((region_count,)),
            dma((group_count,)),
            dma((group_count,)),
        ],
        compiler_params=pltpu.CompilerParams(collective_id=0, has_side_effects=True),
    )(ensemble, tiles, tile_live, observed, perturb, obs_var)


def solution(mesh):
    return jax.shard_map(
        on_device,
        mesh=mesh,
        in_specs=(
            P(("region", "group"), None),
            P(None, None, ("region", "group")),
            P(),
            P(),
            P(),
            P(),
        ),
        out_specs=P(("region", "group"), None),
        check_vma=False,
    )
```

time: 254 us -> 29.6 us (0.12)
  waiting for transfers between devices: 154 us -> 0 us
  blocking collectives: 62 us -> 0 us
  Pallas kernels: 0 us -> 27.7 us
  between operations: 16 us -> 0.01 us
  matrix products: 13.9 us -> 0 us
  other arithmetic: 4.28 us -> 0 us
    psum x2 -> x0, waiting for transfers between devices: 109 us -> none  [on_device(): share = lax.psum(within, 'region')]
    all_gather x4 -> x0, blocking collectives: 62 us -> none  [the longest x2 32.1 us: on_device(): lax.all_gather(innov_share, 'group', axis=0, tiled=True)]
    reduce_scatter x2 -> x0, waiting for transfers between devices: 44.4 us -> none  [on_device(): lax.psum_scatter(partial_value, 'group', scatter_dimension=0, tiled=True)]
    pallas_call x0 -> x1, Pallas kernels: none -> 27.7 us  [on_device(): pl.pallas_call(functools.partial(kernel, region_count, group_count), out_...]
    dot_general x24 -> x0, matrix products: 13.9 us -> none  [the longest x8 4.4 us: newton_weights(): inner = 2.0 * ident - jnp.dot(cov, approx, precision=lax.Precision.HIGHEST)]
  transfers between devices with their start and end apart: 4 -> 0, of which waited for: 4 -> 0; matrix products, arithmetic and copies ran while one was open for 0% -> 0% of each run, Pallas kernels for 0% -> 0%
where the time goes in v1:
time: 29.6 us; the launch traced here: 29.4 us
  Pallas kernels  27.7 us (94%)
  local copies, waits for them, and re-layouts  1.67 us (6%)
    pallas_call x1, Pallas kernels, on_device(): pl.pallas_call(functools.partial(kernel, region_count, group_count), out_...  27.7 us
    unnamed x1, local copies, waits for them, and re-layouts  1.67 us

profile of v1, /device:TPU:0, one launch (start us, length us, event | category | flops | bytes accessed | tf_op | source)
XLA Modules:
  0.0 29.4 jit_solution(12445092832086387323)
XLA Ops:
  0.0 27.7 %shard_map.64 = bf16[256,512]{1,0:T(8,128)(2,1)} custom-call(bf16[256,512]{1,0:T(8,128)(2,1)} %ens_hbm.1, bf16[2,256,256]{2,1,0:T(8,128)(2,1)} %tiles_hbm.1, s32[2,8]{1,0:T(2,128)} %live_ref.1, f32[2,256]{1,0:T(2,128)} %obs_ref.1, bf16[2,256,512]{2,1,0:T(8,128)(2,1)} %pert_hbm.1, f32[2,256]{1,0:T(2,128)} %var_ref.1), custom_call_target="tpu_custom_call" | custom-call | tf_op jit(solution)/shard_map/pallas_call | solution.py:211
  27.7 1.7 %copy.8 = bf16[256,512]{1,0:T(8,128)(2,1)} copy(bf16[256,512]{1,0:T(8,128)(2,1)} %shard_map.64) | data formatting | bytes 524288

commit v2 on v1

--- a/solution.py
+++ b/solution.py
@@ -8,6 +8,8 @@
 from jax.sharding import PartitionSpec as P
 
 NEWTON = 4
+CORES = 2
+PIECES = 2
 F32 = jnp.float32
 BF16 = jnp.bfloat16
 
@@ -33,8 +35,9 @@
     out_ref,
     ens, tiles, pert, partial, rs_buf, z_send, z_buf, spread_buf,
     mean_part, mean_rs, mean_zsend, mean_z,
+    pair_buf, half_buf,
     load_sem, rs_ssem, rs_rsem, z_ssem, z_rsem, ag_ssem, ag_rsem,
-    mrs_ssem, mrs_rsem, mz_ssem, mz_rsem,
+    mrs_ssem, mrs_rsem, mz_ssem, mz_rsem, pair_ssem, pair_rsem,
 ):
     batches, obs_count, members = pert.shape
     region = lax.axis_index("region")
@@ -51,7 +54,7 @@
     loads = [pltpu.make_async_copy(ens_hbm, ens, load_sem.at[0])]
     loads += [pltpu.make_async_copy(tiles_hbm.at[b], tiles.at[b], load_sem.at[1 + b]) for b in range(batches)]
     loads += [pltpu.make_async_copy(pert_hbm.at[b], pert.at[b], load_sem.at[1 + batches + b]) for b in range(batches)]
-    for load in loads:
+    for load in loads[:1 + batches]:
         load.start()
 
     row_at = lax.broadcasted_iota(jnp.int32, (obs_count, obs_count), 0)
@@ -65,11 +68,23 @@
     def as_column(row):
         return jnp.sum(jnp.where(on_diag, row, 0.0), axis=1, keepdims=True)
 
-    def chunk(ref, index):
+    piece_cols = chunk_cols // PIECES
+
+    def chunk(ref, index, piece=None):
         rows = pl.ds(pl.multiple_of(lax.div(index, across) * chunk_rows, chunk_rows), chunk_rows)
-        if across == 1:
-            return ref.at[rows, :]
-        return ref.at[rows, pl.ds(pl.multiple_of(lax.rem(index, across) * chunk_cols, chunk_cols), chunk_cols)]
+        start, width = (0, chunk_cols) if piece is None else (piece * piece_cols, piece_cols)
+        if across > 1:
+            start = pl.multiple_of(lax.rem(index, across) * chunk_cols + start, piece_cols)
+        return ref.at[rows, pl.ds(start, width)]
+
+    def part(ref, piece):
+        return ref if piece is None else ref.at[:, pl.ds(piece * piece_cols, piece_cols)]
+
+    def sem_row(b, piece):
+        return b * PIECES + (piece or 0)
+
+    def pieces_of(b):
+        return range(PIECES) if b == 0 else (None,)
 
     def remote(src, dst, ssem, rsem, where):
         return pltpu.make_async_remote_copy(
@@ -91,49 +106,87 @@
         value = value * live_ref[b, region].astype(F32)
         mean = jnp.mean(value, axis=1, keepdims=True)
         partial[b] = (value - mean).astype(BF16)
-        mean_part[:, b * obs_count:(b + 1) * obs_count] = as_row(mean)
-
-    def scatter(b):
+        return mean
+
+    chips = region_count // CORES
+    chip, core = lax.div(region, CORES), lax.rem(region, CORES)
+    chip_order = [lax.rem(chip + 1 + k, chips) for k in range(chips)]
+    chip_peers = chip_order[:-1]
+    partner = chip * CORES + (CORES - 1 - core)
+
+    def scatter(b, piece):
+        row = sem_row(b, piece)
         for k, peer in enumerate(region_peers):
-            launch(remote(chunk(partial.at[b], peer), rs_buf.at[b, region], rs_ssem.at[b, k], rs_rsem.at[b, region], (peer, group)))
-
-    def sum_region(b):
-        total = chunk(partial.at[b], region)[...].astype(F32)
-        for peer in region_peers:
-            remote(rs_buf.at[b, peer], rs_buf.at[b, peer], rs_ssem.at[b, 0], rs_rsem.at[b, peer], (peer, group)).wait_recv()
-            total = total + rs_buf[b, peer].astype(F32)
-        z_send[b] = total.astype(BF16)
+            launch(remote(chunk(partial.at[b], peer, piece), part(rs_buf.at[b, region], piece), rs_ssem.at[row, k], rs_rsem.at[row, region], (peer, group)))
+
+    def scatter_pair(b):
+        for k, there in enumerate(chip_order):
+            launch(remote(chunk(partial.at[b], there * CORES + CORES - 1 - core), pair_buf.at[b, there], pair_ssem.at[b, k], pair_rsem.at[b, there], (partner, group)))
+
+    def pair_sum(b, there):
+        remote(pair_buf.at[b, there], pair_buf.at[b, there], pair_ssem.at[b, 0], pair_rsem.at[b, there], (partner, group)).wait_recv()
+        return chunk(partial.at[b], there * CORES + core)[...].astype(F32) + pair_buf[b, there].astype(F32)
+
+    def scatter_chips(b):
+        row = sem_row(b, None)
+        for k, there in enumerate(chip_peers):
+            half_buf[b, there] = pair_sum(b, there).astype(BF16)
+            launch(remote(half_buf.at[b, there], rs_buf.at[b, region], rs_ssem.at[row, k], rs_rsem.at[row, region], (there * CORES + core, group)))
+
+    def sum_region(b, piece):
+        row = sem_row(b, piece)
+        if b == 0:
+            total, peers = chunk(partial.at[b], region, piece)[...].astype(F32), region_peers
+        else:
+            total, peers = pair_sum(b, chip), [there * CORES + core for there in chip_peers]
+        for peer in peers:
+            block = part(rs_buf.at[b, peer], piece)
+            remote(block, block, rs_ssem.at[row, 0], rs_rsem.at[row, peer], (peer, group)).wait_recv()
+            total = total + block[...].astype(F32)
+        mine = part(z_send.at[b], piece)
+        mine[...] = total.astype(BF16)
         for k, peer in enumerate(group_peers):
-            launch(remote(z_send.at[b], z_buf.at[b, group], z_ssem.at[b, k], z_rsem.at[b, group], (region, peer)))
-
-    def sum_group(b):
-        total = z_send[b].astype(F32)
+            launch(remote(mine, part(z_buf.at[b, group], piece), z_ssem.at[row, k], z_rsem.at[row, group], (region, peer)))
+
+    def sum_group(b, piece):
+        row = sem_row(b, piece)
+        total = part(z_send.at[b], piece)[...].astype(F32)
         for peer in group_peers:
-            remote(z_buf.at[b, peer], z_buf.at[b, peer], z_ssem.at[b, 0], z_rsem.at[b, peer], (region, peer)).wait_recv()
-            total = total + z_buf[b, peer].astype(F32)
-        mine = chunk(spread_buf.at[b], region)
+            block = part(z_buf.at[b, peer], piece)
+            remote(block, block, z_ssem.at[row, 0], z_rsem.at[row, peer], (region, peer)).wait_recv()
+            total = total + block[...].astype(F32)
+        mine = chunk(spread_buf.at[b], region, piece)
         mine[...] = total.astype(BF16)
         for k, peer in enumerate(region_peers):
-            launch(remote(mine, mine, ag_ssem.at[b, k], ag_rsem.at[b, region], (peer, group)))
+            launch(remote(mine, mine, ag_ssem.at[row, k], ag_rsem.at[row, region], (peer, group)))
 
     def gathered(b):
-        for peer in region_peers:
-            block = chunk(spread_buf.at[b], peer)
-            remote(block, block, ag_ssem.at[b, 0], ag_rsem.at[b, peer], (peer, group)).wait_recv()
+        for piece in pieces_of(b):
+            for peer in region_peers:
+                block = chunk(spread_buf.at[b], peer, piece)
+                row = sem_row(b, piece)
+                remote(block, block, ag_ssem.at[row, 0], ag_rsem.at[row, peer], (peer, group)).wait_recv()
         return spread_buf[b]
 
     loads[0].wait()
-    local_partial(0)
+    means = [local_partial(0)]
     pl.semaphore_wait(barrier, region_count - 1 + group_count - 1)
-    scatter(0)
-    for b in range(1, batches):
-        local_partial(b)
+    for piece in pieces_of(0):
+        scatter(0, piece)
+    for load in loads[1 + batches:]:
+        load.start()
+    for b in range(1, batches):
+        means.append(local_partial(b))
+    for b in range(1, batches):
+        scatter_pair(b)
+    for b in range(batches):
+        mean_part[:, b * obs_count:(b + 1) * obs_count] = as_row(means[b])
     for k, peer in enumerate(region_peers):
         launch(remote(mean_part, mean_rs.at[region], mrs_ssem.at[k], mrs_rsem.at[region], (peer, group)))
     for b in range(1, batches):
-        scatter(b)
-
-    sum_region(0)
+        scatter_chips(b)
+    for piece in pieces_of(0):
+        sum_region(0, piece)
     total = mean_part[...]
     for peer in region_peers:
         remote(mean_rs.at[peer], mean_rs.at[peer], mrs_ssem.at[0], mrs_rsem.at[peer], (peer, group)).wait_recv()
@@ -142,14 +195,15 @@
     for k, peer in enumerate(group_peers):
         launch(remote(mean_zsend, mean_z.at[group], mz_ssem.at[k], mz_rsem.at[group], (region, peer)))
     for b in range(1, batches):
-        sum_region(b)
-    sum_group(0)
+        sum_region(b, None)
+    for piece in pieces_of(0):
+        sum_group(0, piece)
     mean_row = mean_zsend[...]
     for peer in group_peers:
         remote(mean_z.at[peer], mean_z.at[peer], mz_ssem.at[0], mz_rsem.at[peer], (region, peer)).wait_recv()
         mean_row = mean_row + mean_z[peer]
     for b in range(1, batches):
-        sum_group(b)
+        sum_group(b, None)
 
     def anomaly(wide):
         return (wide - jnp.mean(wide, axis=1, keepdims=True)).astype(BF16)
@@ -210,7 +264,7 @@
     dma = pltpu.SemaphoreType.DMA
     return pl.pallas_call(
         functools.partial(kernel, region_count, group_count),
-        out_shape=jax.ShapeDtypeStruct(ensemble.shape, ensemble.dtype),
+        out_shape=pltpu.VMEM(ensemble.shape, ensemble.dtype),
         in_specs=[hbm, hbm, pl.BlockSpec(memory_space=pltpu.SMEM), vmem, hbm, vmem],
         out_specs=vmem,
         scratch_shapes=[
@@ -226,17 +280,21 @@
             pltpu.VMEM((region_count, 1, batches * obs_count), F32),
             pltpu.VMEM((1, batches * obs_count), F32),
             pltpu.VMEM((group_count, 1, batches * obs_count), F32),
+            pltpu.VMEM((batches, region_count // CORES, *block), BF16),
+            pltpu.VMEM((batches, region_count // CORES, *block), BF16),
             dma((1 + 2 * batches,)),
-            dma((batches, region_count)),
-            dma((batches, region_count)),
-            dma((batches, group_count)),
-            dma((batches, group_count)),
-            dma((batches, region_count)),
-            dma((batches, region_count)),
+            dma((batches * PIECES, region_count)),
+            dma((batches * PIECES, region_count)),
+            dma((batches * PIECES, group_count)),
+            dma((batches * PIECES, group_count)),
+            dma((batches * PIECES, region_count)),
+            dma((batches * PIECES, region_count)),
             dma((region_count,)),
             dma((region_count,)),
             dma((group_count,)),
             dma((group_count,)),
+            dma((batches, region_count // CORES)),
+            dma((batches, region_count // CORES)),
         ],
         compiler_params=pltpu.CompilerParams(collective_id=0, has_side_effects=True),
     )(ensemble, tiles, tile_live, observed, perturb, obs_var)

time: 29.6 us -> 27.7 us (0.936)
  local copies, waits for them, and re-layouts: 1.67 us -> 0.71 us
  Pallas kernels: 27.7 us -> 26.9 us
    unnamed x1, local copies, waits for them, and re-layouts: 1.67 us -> 0.71 us
    pallas_call x1, Pallas kernels: 27.7 us -> 26.9 us  [on_device(): pl.pallas_call(functools.partial(kernel, region_count, group_count), out_...]
where the time goes in v2:
time: 27.7 us; the launch traced here: 27.6 us
  Pallas kernels  26.9 us (97%)
  local copies, waits for them, and re-layouts  0.71 us (3%)
    pallas_call x1, Pallas kernels, on_device(): pl.pallas_call(functools.partial(kernel, region_count, group_count), out_...  26.9 us
    unnamed x1, local copies, waits for them, and re-layouts  0.71 us

profile of v2, /device:TPU:0, one launch (start us, length us, event | category | flops | bytes accessed | tf_op | source)
XLA Modules:
  0.0 27.6 jit_solution(10085274268556726268)
XLA Ops:
  0.0 26.9 %shard_map.64 = bf16[256,512]{1,0:T(8,128)(2,1)S(1)} custom-call(bf16[256,512]{1,0:T(8,128)(2,1)} %ens_hbm.1, bf16[2,256,256]{2,1,0:T(8,128)(2,1)} %tiles_hbm.1, s32[2,8]{1,0:T(2,128)} %live_ref.1, f32[2,256]{1,0:T(2,128)} %obs_ref.1, bf16[2,256,512]{2,1,0:T(8,128)(2,1)} %pert_hbm.1, f32[2,256]{1,0:T(2,128)} %var_ref.1), custom_call_target="tpu_custom_call" | custom-call | tf_op jit(solution)/shard_map/pallas_call | solution.py:265
  26.9 0.7 %copy.8 = bf16[256,512]{1,0:T(8,128)(2,1)} copy(bf16[256,512]{1,0:T(8,128)(2,1)S(1)} %shard_map.64) | data formatting | bytes 524288
